TPU v7x, 512 devices: a whole 4x4x16 slice. The times are simulated.
512 devices in a mesh: group: 4 (over y), lat: 16 (over z_hi, x), lon: 8 (over z_lo, core).
Axes of the slice: x: 4, y: 4, z: 16 (z_hi: 4, z_lo: 4; z = z_hi * 4 + z_lo), core: 2. Of those that a mesh axis runs over, the one named last changes fastest.
Arguments:
- species_amounts: float32 [128, 4, 256, 1024], P('group', None, 'lat', 'lon'), may hold values from -4 to 4
- zonal_cell_fraction: float32 [4, 256, 1024], P('group', 'lat', 'lon'), may hold values from -0.3 to 0.3
- meridional_cell_fraction: float32 [4, 256, 1024], P('group', 'lat', 'lon'), may hold values from -0.3 to 0.3
- updraft_cell_fraction: float32 [4, 256, 1024], P('group', 'lat', 'lon'), may hold values from -0.3 to 0.3
- warmth_anomaly: float32 [4, 256, 1024], P('group', 'lat', 'lon'), may hold values from -2 to 2
- mass_per_volume: float32 [4, 256, 1024], P('group', 'lat', 'lon'), may hold values from 0.5 to 2
- chemistry_iterations: int32 [256, 1024], P('lat', 'lon'), may hold values from 1 to 2, as said below
- companion_species: bfloat16 [512, 128], replicated, may hold values from -0.5 to 0.5
- stoichiometric_rate: bfloat16 [128, 512], replicated, may hold values from -0.25 to 0.25
- heat_yield: float32 [128], replicated, may hold values from -0.5 to 0.5
Outputs:
- tracers_out: float32 [128, 4, 256, 1024], P('group', None, 'lat', 'lon')
- east_out: float32 [4, 256, 1024], P('group', 'lat', 'lon')
- north_out: float32 [4, 256, 1024], P('group', 'lat', 'lon')
- temp_out: float32 [4, 256, 1024], P('group', 'lat', 'lon')
Inputs may be any that keep to these rules, and one draw needn't show every extreme that they name: `chemistry_iterations`: columns at latitude rows 192 and above hold 1 or 2, and the last row holds 2; all other columns hold 1.
All inputs are finite; a program needn't handle non-finite values.
Results may differ from a plain program's by a relative error of at most 0.0011.
Values sent between devices are 32-bit elements; how exact they have to be, the bound alone decides.
A program may use at most 64 MiB of HBM per device.

v0:
```python
import jax
import jax.numpy as jnp
from jax import lax
from jax.sharding import PartitionSpec as P

diffusion = 0.1
pressure = 0.05
chem_step = 0.2
block_cells = 512


def cut_along(value, dim, devices):
    lengths = value.shape
    pieces = value.reshape(*lengths[:dim], devices, lengths[dim] // devices, *lengths[dim + 1 :])
    return jnp.moveaxis(pieces, dim, 0)


def joined_along(pieces, dim):
    lengths = list(pieces.shape[1:])
    lengths[dim] *= pieces.shape[0]
    return jnp.moveaxis(pieces, 0, dim).reshape(lengths)


def one_exchange(value, axis, axes, splits, concats):
    sizes = [lax.axis_size(a) for a in axes]
    pieces = cut_along(value, splits[0], sizes[0])
    pieces = jnp.moveaxis(cut_along(pieces, splits[1] + 1, sizes[1]), 0, 1)
    inside = pieces.shape[2:]
    pieces = pieces.reshape(-1, *inside)
    pieces = lax.all_to_all(pieces, axis, split_axis=0, concat_axis=0, tiled=True)
    pieces = joined_along(pieces.reshape(*sizes, *inside), concats[0] + 1)
    return joined_along(pieces, concats[1])


def extended(value, sides, width):
    edges = {}
    for axis, dim in sides:
        devices, length = (lax.axis_size(axis), value.shape[dim])
        up = [(i, (i + 1) % devices) for i in range(devices - 1)]
        last = lax.slice_in_dim(value, length - width, length, axis=dim)
        leading = lax.slice_in_dim(value, 0, width, axis=dim)
        edges[dim] = (
            lax.ppermute(last, axis, up),
            lax.ppermute(leading, axis, [(b, a) for a, b in up]),
        )
    done = []
    for _, dim in sides:
        low, high = edges[dim]
        around = [(width, width) if d in done else (0, 0) for d in range(value.ndim)]
        value = jnp.concatenate([jnp.pad(low, around), value, jnp.pad(high, around)], axis=dim)
        done.append(dim)
    return value


def transport(padded, east_pad, north_pad, upward):
    zonal_cells = padded[..., 1:-1, :]
    zonal_wind = east_pad[:, 1:-1, :]
    face_wind = 0.5 * (zonal_wind[..., :-1] + zonal_wind[..., 1:])
    face_flux = (
        jnp.maximum(face_wind, 0.0) * zonal_cells[..., :-1]
        + jnp.minimum(face_wind, 0.0) * zonal_cells[..., 1:]
    )
    change = face_flux[..., 1:] - face_flux[..., :-1]
    north_cells = padded[..., 1:-1]
    north_wind = north_pad[:, :, 1:-1]
    face_wind = 0.5 * (north_wind[:, :-1] + north_wind[:, 1:])
    face_flux = (
        jnp.maximum(face_wind, 0.0) * north_cells[..., :-1, :]
        + jnp.minimum(face_wind, 0.0) * north_cells[..., 1:, :]
    )
    change = change + (face_flux[..., 1:, :] - face_flux[..., :-1, :])
    centre = padded[..., 1:-1, 1:-1]
    face_wind = 0.5 * (upward[:-1] + upward[1:])
    face_flux = (
        jnp.maximum(face_wind, 0.0) * centre[..., :-1, :, :]
        + jnp.minimum(face_wind, 0.0) * centre[..., 1:, :, :]
    )
    closed = jnp.zeros_like(face_flux[..., :1, :, :])
    face_flux = jnp.concatenate([closed, face_flux, closed], axis=-3)
    change = change + (face_flux[..., 1:, :, :] - face_flux[..., :-1, :, :])
    return centre - change


def dynamics(padded):
    centre = padded[:, :, 1:-1, 1:-1]
    eastern = padded[:, :, 1:-1, 2:]
    western = padded[:, :, 1:-1, :-2]
    northern = padded[:, :, 2:, 1:-1]
    southern = padded[:, :, :-2, 1:-1]
    laplace = eastern + western + northern + southern - 4.0 * centre
    diffused = centre + diffusion * laplace
    zonal_axis_name = diffused[0] - pressure * (eastern[2] - western[2])
    meridional_axis_name = diffused[1] - pressure * (northern[2] - southern[2])
    return (zonal_axis_name, meridional_axis_name, diffused[2])


def react_block(
    tracer_block, rate_block, count_block, companion_species, stoichiometric_rate, heat_yield
):
    species = tracer_block.shape[0]
    width = tracer_block.shape[1]
    repeats = companion_species.shape[0] // species
    deepest = jnp.max(count_block)

    def keep_going(state_pair):
        return state_pair[0] < deepest

    def substep(state_pair):
        counter, current = state_pair
        narrow = current.astype(jnp.bfloat16)
        pair_terms = jnp.dot(companion_species, narrow, preferred_element_type=jnp.float32)
        quadratic = (
            (pair_terms.reshape(repeats, species, width) * current[None])
            .reshape(repeats * species, width)
            .astype(jnp.bfloat16)
        )
        tendency = (
            rate_block[None]
            * jnp.dot(stoichiometric_rate, quadratic, preferred_element_type=jnp.float32)
            - current
        )
        current = jnp.where(counter < count_block[None], current + chem_step * tendency, current)
        return (counter + 1, current)

    final = lax.while_loop(keep_going, substep, (jnp.zeros((), jnp.int32), tracer_block))[1]
    heating = jnp.dot(heat_yield[None], final - tracer_block, precision=lax.Precision.HIGHEST)[0]
    return (final, heating)


def react_cells(
    tracer_cells, rate_cells, count_cells, companion_species, stoichiometric_rate, heat_yield
):
    cell_count = tracer_cells.shape[1]
    sort_order = jnp.argsort(-count_cells, stable=True)
    inverse = jnp.argsort(sort_order)
    sorted_tracers = jnp.take(tracer_cells, sort_order, axis=1)
    sorted_rates = jnp.take(rate_cells, sort_order)
    sorted_counts = jnp.take(count_cells, sort_order)

    def one_block(block_index, outputs):
        offset = block_index * block_cells
        tracer_block = lax.dynamic_slice_in_dim(sorted_tracers, offset, block_cells, 1)
        rate_block = lax.dynamic_slice_in_dim(sorted_rates, offset, block_cells, 0)
        count_block = lax.dynamic_slice_in_dim(sorted_counts, offset, block_cells, 0)
        final, heating = react_block(
            tracer_block,
            rate_block,
            count_block,
            companion_species,
            stoichiometric_rate,
            heat_yield,
        )
        return (
            lax.dynamic_update_slice_in_dim(outputs[0], final, offset, 1),
            lax.dynamic_update_slice_in_dim(outputs[1], heating, offset, 0),
        )

    reacted, heated = lax.fori_loop(
        0,
        cell_count // block_cells,
        one_block,
        (jnp.zeros_like(sorted_tracers), jnp.zeros_like(sorted_rates)),
    )
    return (jnp.take(reacted, inverse, axis=1), jnp.take(heated, inverse))


def scattered(
    advected,
    reaction_rate,
    chemistry_iterations,
    companion_species,
    stoichiometric_rate,
    heat_yield,
):
    groups = lax.axis_size("group")
    own_group = lax.axis_index("group")
    stratum_total = advected.shape[1]
    meridian_span = advected.shape[2]
    parallel_span = advected.shape[3]
    column_part = parallel_span // groups
    count_field = jnp.broadcast_to(
        chemistry_iterations.astype(jnp.float32)[None],
        (stratum_total, meridian_span, parallel_span),
    )
    own_rates = lax.dynamic_slice_in_dim(reaction_rate, own_group * column_part, column_part, 2)
    own_counts = lax.dynamic_slice_in_dim(count_field, own_group * column_part, column_part, 2)
    cell_info = jnp.concatenate([own_rates, own_counts], axis=2)[None, :, None]
    arrived, info_in = (
        one_exchange(advected[:, :, None], ("group", "lat"), ("group", "lat"), (1, 3), (0, 2)),
        one_exchange(cell_info, ("group", "lat"), ("group", "lat"), (1, 3), (0, 2)),
    )
    species = arrived.shape[0]
    cell_shape = arrived.shape[1:]
    cell_data = info_in.reshape(groups, cell_shape[0], cell_shape[1], cell_shape[2], 2, column_part)
    cell_data = cell_data.transpose(4, 1, 2, 3, 0, 5).reshape(2, -1)
    reacted, heating = react_cells(
        arrived.reshape(species, -1),
        cell_data[0],
        cell_data[1].astype(jnp.int32),
        companion_species,
        stoichiometric_rate,
        heat_yield,
    )
    heat_copies = jnp.broadcast_to(heating.reshape((1,) + cell_shape), (groups,) + cell_shape)
    returned, heat_back = (
        one_exchange(
            reacted.reshape(arrived.shape), ("group", "lat"), ("group", "lat"), (0, 2), (1, 3)
        ),
        one_exchange(heat_copies, ("group", "lat"), ("group", "lat"), (0, 2), (1, 3)),
    )
    return (returned[:, :, 0], heat_back[0, :, 0])


def local(
    species_amounts,
    zonal_cell_fraction,
    meridional_cell_fraction,
    updraft_cell_fraction,
    warmth_anomaly,
    mass_per_volume,
    chemistry_iterations,
    companion_species,
    stoichiometric_rate,
    heat_yield,
):
    own_group = lax.axis_index("group")
    local_strata = warmth_anomaly.shape[0]
    owned_tracers = species_amounts.shape[0]
    columns = lax.all_gather(
        jnp.stack(
            [
                zonal_cell_fraction,
                meridional_cell_fraction,
                updraft_cell_fraction,
                warmth_anomaly,
                mass_per_volume,
            ]
        ),
        "group",
        axis=1,
        tiled=True,
    )
    zonal_axis_name, meridional_axis_name, upward, heat_snapshot, air_density = (
        columns[0],
        columns[1],
        columns[2],
        columns[3],
        columns[4],
    )
    stacked = jnp.concatenate(
        [species_amounts, jnp.stack([zonal_axis_name, meridional_axis_name, heat_snapshot])], axis=0
    )
    padded = extended(stacked, (("lat", 2), ("lon", 3)), 1)
    advected = transport(
        padded[:owned_tracers], padded[owned_tracers], padded[owned_tracers + 1], upward
    )
    new_east, new_north, warmed = dynamics(padded[owned_tracers:])
    reaction_rate = jax.nn.sigmoid(2.0 * heat_snapshot)
    reacted, heating = scattered(
        advected,
        reaction_rate,
        chemistry_iterations,
        companion_species,
        stoichiometric_rate,
        heat_yield,
    )
    heat_snapshot = warmed + heating / air_density
    start_level = own_group * local_strata
    east_mine = lax.dynamic_slice_in_dim(new_east, start_level, local_strata, 0)
    north_mine = lax.dynamic_slice_in_dim(new_north, start_level, local_strata, 0)
    thermal_mine = lax.dynamic_slice_in_dim(heat_snapshot, start_level, local_strata, 0)
    return (reacted, east_mine, north_mine, thermal_mine)


def solution(mesh):
    return jax.shard_map(
        local,
        mesh=mesh,
        in_specs=(
            P("group", None, "lat", "lon"),
            P("group", "lat", "lon"),
            P("group", "lat", "lon"),
            P("group", "lat", "lon"),
            P("group", "lat", "lon"),
            P("group", "lat", "lon"),
            P("lat", "lon"),
            P(),
            P(),
            P(),
        ),
        out_specs=(
            P("group", None, "lat", "lon"),
            P("group", "lat", "lon"),
            P("group", "lat", "lon"),
            P("group", "lat", "lon"),
        ),
        check_vma=False,
    )
```

profile of v0, /device:TPU:2, one launch (start us, length us, event | category | flops | bytes accessed | tf_op | source)
XLA Modules:
  0.0 286.0 jit_solution(10840602657939708706)
XLA Ops:
  4.2 12.6 %all_gather.3 = f32[5,4,16,128]{3,2,1,0:T(8,128)S(1)} all-gather(f32[5,1,16,128]{3,2,1,0:T(8,128)S(1)} %constant_dynamic-update-slice_fusion.1), channel_id=1, replica_groups=mesh['group'=4,'lat'=16,'lon'=8] {'group'}, dimensions={1}, use_global_device_ids=true | all-gather | bytes 204800 | tf_op jit(solution)/shard_map/all_gather | solution.py:229
  19.0 20.6 %all-to-all-start.1 = ((f32[64,1,1,1,1,64]{5,4,3,2,1,0:T(1,128)}), f32[64,1,1,1,1,64]{5,4,3,2,1,0:T(1,128)S(1)}, u32[]{:S(2)}, u32[]{:S(2)}) async-start(f32[64,1,1,1,1,64]{5,4,3,2,1,0:T(1,128)} %bitcast.11), calls=%async_computation.1 | async-start | bytes 65536 | tf_op jit(solution)/shard_map/all_to_all | solution.py:30
  39.6 2.0 pad_maximum_fusion.11
  41.6 3.4 %collective-permute-start.1 = (f32[35,4,1,128]{3,2,1,0:T(1,128)}, f32[35,4,1,128]{3,2,1,0:T(1,128)S(1)}, u32[]{:S(2)}, u32[]{:S(2)}) collective-permute-start(f32[35,4,1,128]{3,2,1,0:T(1,128)} %get-tuple-element.257), channel_id=1, source_target_pairs={{0,8},{8,16},{16,24},{24,32},{32,40},{40,48},{48,56},{56,64},{64,7... | collective-permute-start | bytes 215048 | tf_op jit(solution)/shard_map/ppermute | solution.py:43
  44.9 2.5 collective-permute-start.2
  47.9 1.4 copy.90
  51.4 3.0 %collective-permute-start = (f32[35,4,16,1]{0,2,3,1:T(8,128)S(1)}, f32[35,4,16,1]{0,2,3,1:T(8,128)S(1)}, u32[]{:S(2)}, u32[]{:S(2)}) collective-permute-start(f32[35,4,16,1]{0,2,3,1:T(8,128)S(1)} %copy.88), channel_id=1, source_target_pairs={{0,1},{1,2},{2,3},{3,4},{4,5},{5,6},{6,7},{8,9},{9,10},{10,11},{11... | collective-permute-start | bytes 26888 | tf_op jit(solution)/shard_map/ppermute | solution.py:43
  56.2 2.0 copy.89
  58.2 1.5 pad.9
  59.8 2.0 copy.91
  61.8 1.5 pad.10
  64.5 4.1 %maximum_maximum_fusion = (f32[35,4,18,129]{3,2,1,0:T(8,128)S(1)}, f32[35,4,18,129]{3,2,1,0:T(8,128)S(1)}) fusion(f32[35,4,1,128]{3,2,1,0:T(1,128)} %collective-permute-done.2, f32[1,4,16,128]{3,2,1,0:T(8,128)S(1)} %get-tuple-element.260, f32[2,4,16,128]{3,2,1,0:T(8,128)S(1)} %slice.229, f32[32,4,16,128]{3,2,1,0:T(8,128)S(1)} %copy-done, ...), kind=kLoop, calls=%fused_computation.21 | loop fusion | flops 3250800 | bytes 3911040 | tf_op jit(solution)/shard_map/concatenate | solution.py:50
  72.3 1.6 copy.93
  73.9 21.2 %all-to-all-start = ((f32[64,32,1,1,1,128]{5,1,4,3,2,0:T(8,128)}), f32[64,32,1,1,1,128]{5,1,4,3,2,0:T(8,128)S(1)}, u32[]{:S(2)}, u32[]{:S(2)}) async-start(f32[64,32,1,1,1,128]{5,1,4,3,2,0:T(8,128)} %copy.93), calls=%async_computation | async-start | bytes 2097152 | tf_op jit(solution)/shard_map/all_to_all | solution.py:30
  95.4 5.0 %sort.34 = (s32[2048]{0:T(1024)}, s32[2048]{0:T(1024)S(1)}) sort(s32[2048]{0:T(1024)S(1)} %neg.8, s32[2048]{0:T(1024)S(1)} %iota.8), dimensions={0}, to_apply=%region_0.1 | sort | flops 22528 | bytes 32768 | tf_op jit(solution)/shard_map/jit(argsort)/sort | solution.py:134
  100.5 5.0 %sort.35 = (s32[2048]{0:T(1024)}, s32[2048]{0:T(1024)S(1)}) sort(s32[2048]{0:T(1024)S(1)} %get-tuple-element.201, s32[2048]{0:T(1024)S(1)} %iota.9), dimensions={0}, to_apply=%region_6.9 | sort | flops 22528 | bytes 32768 | tf_op jit(solution)/shard_map/jit(argsort)/sort | solution.py:135
  105.5 11.8 %gather_fusion = s32[2048]{0:T(1024)S(1)} fusion(s32[2048]{0:T(1024)S(1)} %convert_element_type.20, s32[2048]{0:T(1024)S(1)} %get-tuple-element.274), kind=kCustom, calls=%fused_computation.4 | custom fusion | bytes 24576 | tf_op jit(solution)/shard_map/jit(_take)/gather | solution.py:138
  117.3 11.8 %gather_fusion.2 = f32[2048]{0:T(1024)S(1)} fusion(f32[2048]{0:T(1024)S(1)} %squeeze.14, s32[2048]{0:T(1024)S(1)} %get-tuple-element.274), kind=kCustom, calls=%fused_computation.1.clone | custom fusion | bytes 24576 | tf_op jit(solution)/shard_map/jit(_take)/gather | solution.py:137
  129.1 18.6 %all-to-all-done = f32[64,32,1,1,1,128]{5,1,4,3,2,0:T(8,128)S(1)} async-done(((f32[64,32,1,1,1,128]{5,1,4,3,2,0:T(8,128)}), f32[64,32,1,1,1,128]{5,1,4,3,2,0:T(8,128)S(1)}, u32[]{:S(2)}, u32[]{:S(2)}) %all-to-all-start) | async-done | bytes 1048608 | tf_op jit(solution)/shard_map/all_to_all | solution.py:30
  148.2 5.5 %gather_fusion.1 = f32[2048,128]{1,0:T(8,128)S(1)} fusion(f32[128,2048]{0,1:T(8,128)S(1)} %bitcast.130, s32[2048]{0:T(1024)S(1)} %get-tuple-element.274), kind=kCustom, calls=%fused_computation.clone | custom fusion | bytes 2105344 | tf_op jit(solution)/shard_map/jit(_take)/gather | solution.py:136
  156.1 23.4 %while.38 = (s32[]{:T(128)}, f32[128,2048]{0,1:T(8,128)}, f32[2048]{0:T(1024)S(1)}, f32[128,2048]{0,1:T(8,128)}, s32[2048]{0:T(1024)S(1)}, /*index=5*/f32[2048]{...) while((s32[]{:T(128)}, f32[128,2048]{0,1:T(8,128)}, ...), condition=%wide.region_5.8_spmd, body=%wide.region_1.7_spmd.sunk | while | flops 135988224 | bytes 6311812 | solution.py:158
  157.9 4.0 %while.39 = (s32[]{:T(128)}, f32[128,512]{0,1:T(8,128)S(1)}, s32[]{:T(128)}, s32[512]{0:T(512)S(1)}, f32[512]{0:T(512)S(1)}, /*index=5*/bf16[512,128]{1,0:T(8,128)(2,1)S(1)}, bf16[128,512]{1,0:T(8,128)(2,1)S(1)}, s32[]{:T(128)}) while((s32[]{:T(128)}, f32[128,512]{0,1:T(8,128)S(1)}, s32[]{:T(128)}, s32[512]{0:T(512)S(1)}, f32[512]{0:T(512)S(1)}, ...), condition=%wide.region_4.6_spmd, body=%wide.region_3.5_spmd.sunk | while | flops 135135744 | bytes 4199521 | solution.py:125
  165.0 2.3 while.39
  170.4 2.3 while.39
  175.9 2.3 while.39
  179.5 11.8 %gather_fusion.4 = f32[2048]{0:T(1024)S(1)} fusion(f32[2048]{0:T(1024)S(1)} %get-tuple-element.480, s32[2048]{0:T(1024)S(1)} %get-tuple-element.275), kind=kCustom, calls=%fused_computation.3.clone | custom fusion | bytes 24576 | tf_op jit(solution)/shard_map/jit(_take)/gather | solution.py:164
  191.3 5.5 %gather_fusion.3 = f32[2048,128]{1,0:T(8,128)S(1)} fusion(f32[128,2048]{0,1:T(8,128)S(1)} %copy-done.1, s32[2048]{0:T(1024)S(1)} %get-tuple-element.275), kind=kCustom, calls=%fused_computation.2.clone | custom fusion | bytes 2105344 | tf_op jit(solution)/shard_map/jit(_take)/gather | solution.py:164
  197.4 12.2 %all-to-all-start.3 = ((f32[64,1,1,1,1,128]{5,4,3,2,1,0:T(1,128)}), f32[64,1,1,1,1,128]{5,4,3,2,1,0:T(1,128)S(1)}, u32[]{:S(2)}, u32[]{:S(2)}) async-start(f32[64,1,1,1,1,128]{5,4,3,2,1,0:T(1,128)} %bitcast.45), calls=%async_computation.3 | async-start | bytes 65536 | tf_op jit(solution)/shard_map/all_to_all | solution.py:30
  211.7 13.6 %all-to-all-done.3 = f32[64,1,1,1,1,128]{5,4,3,2,1,0:T(1,128)S(1)} async-done(((f32[64,1,1,1,1,128]{5,4,3,2,1,0:T(1,128)}), f32[64,1,1,1,1,128]{5,4,3,2,1,0:T(1,128)S(1)}, u32[]{:S(2)}, u32[]{:S(2)}) %all-to-all-start.3) | async-done | bytes 32800 | tf_op jit(solution)/shard_map/all_to_all | solution.py:30
  225.4 6.3 %all-to-all-start.2 = ((f32[64,32,1,1,1,128]{5,1,4,3,2,0:T(8,128)}), f32[64,32,1,1,1,128]{5,1,4,3,2,0:T(8,128)}, u32[]{:S(2)}, u32[]{:S(2)}) async-start(f32[64,32,1,1,1,128]{5,1,4,3,2,0:T(8,128)} %bitcast.133), calls=%async_computation.2 | async-start | bytes 2097152 | tf_op jit(solution)/shard_map/all_to_all | solution.py:30
  236.0 47.2 %all-to-all-done.2 = f32[64,32,1,1,1,128]{5,1,4,3,2,0:T(8,128)} async-done(((f32[64,32,1,1,1,128]{5,1,4,3,2,0:T(8,128)}), f32[64,32,1,1,1,128]{5,1,4,3,2,0:T(8,128)}, u32[]{:S(2)}, u32[]{:S(2)}) %all-to-all-start.2) | async-done | bytes 1048608 | tf_op jit(solution)/shard_map/all_to_all | solution.py:30
  283.2 2.8 copy.106
  (133 shorter events, 42.4 us)
Async XLA Ops:
  0.6 46.8 %copy-start = (f32[32,4,16,128]{3,2,1,0:T(8,128)S(1)}, f32[32,4,16,128]{3,2,1,0:T(8,128)}, u32[]{:S(2)}) copy-start(f32[32,4,16,128]{3,2,1,0:T(8,128)} %param.18) | copy-start | bytes 3145732
  16.8 30.6 %copy-start.9 = (f32[5,4,16,128]{3,2,1,0:T(8,128)}, f32[5,4,16,128]{3,2,1,0:T(8,128)S(1)}, u32[]{:S(2)}) copy-start(f32[5,4,16,128]{3,2,1,0:T(8,128)S(1)} %all_gather.3) | copy-start | bytes 491524
  19.0 54.9 %all-to-all-start.1 = ((f32[64,1,1,1,1,64]{5,4,3,2,1,0:T(1,128)}), f32[64,1,1,1,1,64]{5,4,3,2,1,0:T(1,128)S(1)}, u32[]{:S(2)}, u32[]{:S(2)}) async-start(f32[64,1,1,1,1,64]{5,4,3,2,1,0:T(1,128)} %bitcast.11), calls=%async_computation.1 | async-start | bytes 65536 | tf_op jit(solution)/shard_map/all_to_all | solution.py:30
  41.6 21.8 %collective-permute-start.1 = (f32[35,4,1,128]{3,2,1,0:T(1,128)}, f32[35,4,1,128]{3,2,1,0:T(1,128)S(1)}, u32[]{:S(2)}, u32[]{:S(2)}) collective-permute-start(f32[35,4,1,128]{3,2,1,0:T(1,128)} %get-tuple-element.257), channel_id=1, source_target_pairs={{0,8},{8,16},{16,24},{24,32},{32,40},{40,48},{48,56},{56,64},{64,7... | collective-permute-start | bytes 215048 | tf_op jit(solution)/shard_map/ppermute | solution.py:43
  44.9 18.4 %collective-permute-start.2 = (f32[35,4,1,128]{3,2,1,0:T(1,128)}, f32[35,4,1,128]{3,2,1,0:T(1,128)}, u32[]{:S(2)}, u32[]{:S(2)}) collective-permute-start(f32[35,4,1,128]{3,2,1,0:T(1,128)} %get-tuple-element.258), channel_id=1, source_target_pairs={{8,0},{16,8},{24,16},{32,24},{40,32},{48,40},{56,48},{64,56},{72,6... | collective-permute-start | bytes 215048 | tf_op jit(solution)/shard_map/ppermute | solution.py:44
  49.3 10.5 %collective-permute-start.3 = (f32[35,4,16,1]{0,2,3,1:T(8,128)}, f32[35,4,16,1]{0,2,3,1:T(8,128)S(1)}, u32[]{:S(2)}, u32[]{:S(2)}) collective-permute-start(f32[35,4,16,1]{0,2,3,1:T(8,128)} %copy.90), channel_id=1, source_target_pairs={{1,0},{2,1},{3,2},{4,3},{5,4},{6,5},{7,6},{9,8},{10,9},{11,10},{12... | collective-permute-start | bytes 26888 | tf_op jit(solution)/shard_map/ppermute | solution.py:44
  51.4 4.8 %collective-permute-start = (f32[35,4,16,1]{0,2,3,1:T(8,128)S(1)}, f32[35,4,16,1]{0,2,3,1:T(8,128)S(1)}, u32[]{:S(2)}, u32[]{:S(2)}) collective-permute-start(f32[35,4,16,1]{0,2,3,1:T(8,128)S(1)} %copy.88), channel_id=1, source_target_pairs={{0,1},{1,2},{2,3},{3,4},{4,5},{5,6},{6,7},{8,9},{9,10},{10,11},{11... | collective-permute-start | bytes 26888 | tf_op jit(solution)/shard_map/ppermute | solution.py:43
  59.8 4.7 %copy-start.4 = (f32[35,4,18,1]{3,2,1,0:T(8,128)}, f32[35,4,18,1]{3,2,1,0:T(8,128)S(1)}, u32[]{:S(2)}) copy-start(f32[35,4,18,1]{3,2,1,0:T(8,128)S(1)} %pad.9) | copy-start | bytes 30244
  63.3 1.2 copy-start.6
  70.6 1.1 copy-start.8
  73.9 73.8 %all-to-all-start = ((f32[64,32,1,1,1,128]{5,1,4,3,2,0:T(8,128)}), f32[64,32,1,1,1,128]{5,1,4,3,2,0:T(8,128)S(1)}, u32[]{:S(2)}, u32[]{:S(2)}) async-start(f32[64,32,1,1,1,128]{5,1,4,3,2,0:T(8,128)} %copy.93), calls=%async_computation | async-start | bytes 2097152 | tf_op jit(solution)/shard_map/all_to_all | solution.py:30
  153.6 2.4 copy-start.2
  153.6 2.4 copy-start.3
  153.7 2.4 copy-start.10
  179.5 11.8 %copy-start.1 = (f32[128,2048]{0,1:T(8,128)S(1)}, f32[128,2048]{0,1:T(8,128)}, u32[]{:S(2)}) copy-start(f32[128,2048]{0,1:T(8,128)} %get-tuple-element.479) | copy-start | bytes 3145732
  197.4 28.0 %all-to-all-start.3 = ((f32[64,1,1,1,1,128]{5,4,3,2,1,0:T(1,128)}), f32[64,1,1,1,1,128]{5,4,3,2,1,0:T(1,128)S(1)}, u32[]{:S(2)}, u32[]{:S(2)}) async-start(f32[64,1,1,1,1,128]{5,4,3,2,1,0:T(1,128)} %bitcast.45), calls=%async_computation.3 | async-start | bytes 65536 | tf_op jit(solution)/shard_map/all_to_all | solution.py:30
  211.7 20.0 %copy-start.5 = (f32[35,4,18,1]{3,2,1,0:T(8,128)S(1)}, f32[35,4,18,1]{3,2,1,0:T(8,128)}, u32[]{:S(2)}) copy-start(f32[35,4,18,1]{3,2,1,0:T(8,128)} %copy-done.4) | copy-start | bytes 30244
  225.4 57.8 %all-to-all-start.2 = ((f32[64,32,1,1,1,128]{5,1,4,3,2,0:T(8,128)}), f32[64,32,1,1,1,128]{5,1,4,3,2,0:T(8,128)}, u32[]{:S(2)}, u32[]{:S(2)}) async-start(f32[64,32,1,1,1,128]{5,1,4,3,2,0:T(8,128)} %bitcast.133), calls=%async_computation.2 | async-start | bytes 2097152 | tf_op jit(solution)/shard_map/all_to_all | solution.py:30
  231.8 1.6 copy-start.7
where the time goes:
time: 287 us; the launch traced here: 286 us
  local copies, waits for them, and re-layouts  79.4 us (28%)
  waiting for transfers between devices  79.4 us (28%)
  starting transfers between devices  70.3 us (24%)
  other arithmetic  32 us (11%)
  blocking collectives  12.6 us (4%)
  loops' own time  6.19 us (2%)
  matrix products  4.96 us (2%)
    all_to_all x4, waiting for transfers between devices, one_exchange(): lax.all_to_all(pieces, axis, split_axis=0, concat_axis=0, tiled=True)  79.4 us
    all_to_all x4, starting transfers between devices, one_exchange(): lax.all_to_all(pieces, axis, split_axis=0, concat_axis=0, tiled=True)  60.2 us
    gather x2, local copies, waits for them, and re-layouts, react_cells(): return (jnp.take(reacted, inverse, axis=1), jnp.take(heated, inverse))  17.2 us
    all_gather x1, blocking collectives, local(): lax.all_gather(jnp.stack([zonal_cell_fraction, meridional_cell_fraction,...  12.6 us
    gather x1, local copies, waits for them, and re-layouts, react_cells(): sorted_rates = jnp.take(rate_cells, sort_order)  11.8 us
    gather x1, local copies, waits for them, and re-layouts, react_cells(): sorted_counts = jnp.take(count_cells, sort_order)  11.8 us
    ppermute x2, starting transfers between devices, extended(): lax.ppermute(last, axis, up)  6.38 us
    another operation x4, loops' own time, react_block(): lax.while_loop(keep_going, substep, (jnp.zeros((), jnp.int32), tracer_blo...  6.09 us
  transfers between devices with their start and end apart: 8, of which 3 were waited for; matrix products, arithmetic and copies ran while one was open for 22% of the time, Pallas kernels for 0%

commit v1 on v0

--- a/solution.py
+++ b/solution.py
@@ -226,19 +226,27 @@
     own_group = lax.axis_index("group")
     local_strata = warmth_anomaly.shape[0]
     owned_tracers = species_amounts.shape[0]
-    columns = lax.all_gather(
-        jnp.stack(
-            [
-                zonal_cell_fraction,
-                meridional_cell_fraction,
-                updraft_cell_fraction,
-                warmth_anomaly,
-                mass_per_volume,
-            ]
+    columns = jnp.concatenate(
+        lax.all_to_all(
+            jnp.stack(
+                [
+                    jnp.stack(
+                        [
+                            zonal_cell_fraction,
+                            meridional_cell_fraction,
+                            updraft_cell_fraction,
+                            warmth_anomaly,
+                            mass_per_volume,
+                        ]
+                    )
+                ]
+                * lax.axis_size("group")
+            ),
+            "group",
+            0,
+            0,
         ),
-        "group",
         axis=1,
-        tiled=True,
     )
     zonal_axis_name, meridional_axis_name, upward, heat_snapshot, air_density = (
         columns[0],

time: 287 us -> 293 us (1.021)
  the two profiles are of different devices: /device:TPU:2 before, /device:TPU:32 now
where the time goes in v1:
time: 293 us; the launch traced here: 292 us
  waiting for transfers between devices  93.9 us (32%)
  local copies, waits for them, and re-layouts  82.6 us (28%)
  starting transfers between devices  65.9 us (22%)
  other arithmetic  36.9 us (13%)
  loops' own time  6.19 us (2%)
  matrix products  4.96 us (2%)
    all_to_all x4, waiting for transfers between devices, one_exchange(): lax.all_to_all(pieces, axis, split_axis=0, concat_axis=0, tiled=True)  85.8 us
    all_to_all x4, starting transfers between devices, one_exchange(): lax.all_to_all(pieces, axis, split_axis=0, concat_axis=0, tiled=True)  51.8 us
    gather x2, local copies, waits for them, and re-layouts, react_cells(): return (jnp.take(reacted, inverse, axis=1), jnp.take(heated, inverse))  17.2 us
    gather x1, local copies, waits for them, and re-layouts, react_cells(): sorted_rates = jnp.take(rate_cells, sort_order)  11.8 us
    gather x1, local copies, waits for them, and re-layouts, react_cells(): sorted_counts = jnp.take(count_cells, sort_order)  11.8 us
    concatenate x3, other arithmetic, extended(): jnp.concatenate([jnp.pad(low, around), value, jnp.pad(high, around)], axi...  10.7 us
    ppermute x2, starting transfers between devices, extended(): lax.ppermute(last, axis, up)  6.43 us
    another operation x4, loops' own time, react_block(): lax.while_loop(keep_going, substep, (jnp.zeros((), jnp.int32), tracer_blo...  6.09 us
  transfers between devices with their start and end apart: 9, of which 5 were waited for; matrix products, arithmetic and copies ran while one was open for 24% of the time, Pallas kernels for 0%

profile of v1, /device:TPU:32, one launch (start us, length us, event | category | flops | bytes accessed | tf_op | source)
XLA Modules:
  0.0 291.7 jit_solution(2447365810936025451)
XLA Ops:
  4.9 4.5 %all-to-all-start = ((f32[4,5,1,16,128]{4,3,2,1,0:T(8,128)}), f32[4,5,1,16,128]{4,3,2,1,0:T(8,128)S(1)}, u32[]{:S(2)}, u32[]{:S(2)}) async-start(f32[4,5,1,16,128]{4,3,2,1,0:T(8,128)} %stack.34), calls=%async_computation | async-start | bytes 327680 | tf_op jit(solution)/shard_map/all_to_all | solution.py:230
  10.1 5.4 %all-to-all-done = f32[4,5,1,16,128]{4,3,2,1,0:T(8,128)S(1)} async-done(((f32[4,5,1,16,128]{4,3,2,1,0:T(8,128)}), f32[4,5,1,16,128]{4,3,2,1,0:T(8,128)S(1)}, u32[]{:S(2)}, u32[]{:S(2)}) %all-to-all-start) | async-done | bytes 163872 | tf_op jit(solution)/shard_map/all_to_all | solution.py:230
  16.8 2.0 pad_maximum_fusion.6
  19.7 18.5 %all-to-all-start.2 = ((f32[64,1,1,1,1,64]{5,4,3,2,1,0:T(1,128)}), f32[64,1,1,1,1,64]{5,4,3,2,1,0:T(1,128)}, u32[]{:S(2)}, u32[]{:S(2)}) async-start(f32[64,1,1,1,1,64]{5,4,3,2,1,0:T(1,128)} %bitcast.12), calls=%async_computation.2 | async-start | bytes 65536 | tf_op jit(solution)/shard_map/all_to_all | solution.py:30
  38.2 4.0 %collective-permute-start.1 = (f32[35,4,1,128]{3,2,1,0:T(1,128)}, f32[35,4,1,128]{3,2,1,0:T(1,128)}, u32[]{:S(2)}, u32[]{:S(2)}) collective-permute-start(f32[35,4,1,128]{3,2,1,0:T(1,128)} %get-tuple-element.253), channel_id=1, source_target_pairs={{0,8},{8,16},{16,24},{24,32},{32,40},{40,48},{48,56},{56,64},{64,7... | collective-permute-start | bytes 215048 | tf_op jit(solution)/shard_map/ppermute | solution.py:43
  45.0 1.9 copy.53
  48.3 1.9 collective-permute-start.3
  50.2 2.4 collective-permute-start
  52.8 2.7 collective-permute-done
  55.5 2.0 copy.54
  59.0 2.8 copy.56
  63.4 4.8 %pad_maximum_fusion = f32[35,4,18,130]{3,2,1,0:T(8,128)S(1)} fusion(f32[35,4,18,1]{3,2,1,0:T(8,128)S(1)} %pad.10, f32[35,4,1,128]{3,2,1,0:T(1,128)} %collective-permute-done.2, f32[1,4,16,128]{3,2,1,0:T(8,128)S(1)} %copy-done.12, f32[1,4,16,128]{3,2,1,0:T(8,128)S(1)} %copy-done.15, f32[1,4,16,128]{3,2,1,0:T(8,128)S(1)} %copy-done.9, ...), kind=kLoop, calls=%fused_computation.21 | loop fusion | flops 2293200 | bytes 2620800 | tf_op jit(solution)/shard_map/concatenate | solution.py:50
  68.5 4.6 %maximum_maximum_fusion = (f32[35,4,18,129]{3,2,1,0:T(8,128)S(1)}, f32[35,4,18,129]{3,2,1,0:T(8,128)S(1)}) fusion(f32[35,4,1,128]{3,2,1,0:T(1,128)} %collective-permute-done.2, f32[1,4,16,128]{3,2,1,0:T(8,128)S(1)} %copy-done.12, f32[1,4,16,128]{3,2,1,0:T(8,128)S(1)} %copy-done.15, f32[1,4,16,128]{3,2,1,0:T(8,128)S(1)} %copy-done.9, ...), kind=kLoop, calls=%fused_computation.22 | loop fusion | flops 3900960 | bytes 3911040 | tf_op jit(solution)/shard_map/concatenate | solution.py:50
  77.7 21.8 %all-to-all-start.1 = ((f32[64,32,1,1,1,128]{5,1,4,3,2,0:T(8,128)}), f32[64,32,1,1,1,128]{5,1,4,3,2,0:T(8,128)S(1)}, u32[]{:S(2)}, u32[]{:S(2)}) async-start(f32[64,32,1,1,1,128]{5,1,4,3,2,0:T(8,128)} %copy.57), calls=%async_computation.1 | async-start | bytes 2097152 | tf_op jit(solution)/shard_map/all_to_all | solution.py:30
  100.6 5.0 %sort.34 = (s32[2048]{0:T(1024)}, s32[2048]{0:T(1024)S(1)}) sort(s32[2048]{0:T(1024)S(1)} %neg.8, s32[2048]{0:T(1024)S(1)} %iota.8), dimensions={0}, to_apply=%region_0.1 | sort | flops 22528 | bytes 32768 | tf_op jit(solution)/shard_map/jit(argsort)/sort | solution.py:134
  105.6 5.0 %sort.35 = (s32[2048]{0:T(1024)}, s32[2048]{0:T(1024)S(1)}) sort(s32[2048]{0:T(1024)S(1)} %get-tuple-element.201, s32[2048]{0:T(1024)S(1)} %iota.9), dimensions={0}, to_apply=%region_6.9 | sort | flops 22528 | bytes 32768 | tf_op jit(solution)/shard_map/jit(argsort)/sort | solution.py:135
  110.7 11.8 %gather_fusion = s32[2048]{0:T(1024)S(1)} fusion(s32[2048]{0:T(1024)S(1)} %convert_element_type.20, s32[2048]{0:T(1024)S(1)} %get-tuple-element.271), kind=kCustom, calls=%fused_computation.4 | custom fusion | bytes 24576 | tf_op jit(solution)/shard_map/jit(_take)/gather | solution.py:138
  122.5 11.8 %gather_fusion.2 = f32[2048]{0:T(1024)S(1)} fusion(f32[2048]{0:T(1024)S(1)} %squeeze.14, s32[2048]{0:T(1024)S(1)} %get-tuple-element.271), kind=kCustom, calls=%fused_computation.1.clone | custom fusion | bytes 24576 | tf_op jit(solution)/shard_map/jit(_take)/gather | solution.py:137
  134.3 21.2 %all-to-all-done.1 = f32[64,32,1,1,1,128]{5,1,4,3,2,0:T(8,128)S(1)} async-done(((f32[64,32,1,1,1,128]{5,1,4,3,2,0:T(8,128)}), f32[64,32,1,1,1,128]{5,1,4,3,2,0:T(8,128)S(1)}, u32[]{:S(2)}, u32[]{:S(2)}) %all-to-all-start.1) | async-done | bytes 1048608 | tf_op jit(solution)/shard_map/all_to_all | solution.py:30
  155.9 5.5 %gather_fusion.1 = f32[2048,128]{1,0:T(8,128)S(1)} fusion(f32[128,2048]{0,1:T(8,128)S(1)} %bitcast.143, s32[2048]{0:T(1024)S(1)} %get-tuple-element.271), kind=kCustom, calls=%fused_computation.clone | custom fusion | bytes 2105344 | tf_op jit(solution)/shard_map/jit(_take)/gather | solution.py:136
  163.8 23.4 %while.38 = (s32[]{:T(128)}, f32[128,2048]{0,1:T(8,128)}, f32[2048]{0:T(1024)S(1)}, f32[128,2048]{0,1:T(8,128)}, s32[2048]{0:T(1024)S(1)}, /*index=5*/f32[2048]{...) while((s32[]{:T(128)}, f32[128,2048]{0,1:T(8,128)}, ...), condition=%wide.region_5.8_spmd, body=%wide.region_1.7_spmd.sunk | while | flops 135988224 | bytes 6311812 | solution.py:158
  165.6 4.0 %while.39 = (s32[]{:T(128)}, f32[128,512]{0,1:T(8,128)S(1)}, s32[]{:T(128)}, s32[512]{0:T(512)S(1)}, f32[512]{0:T(512)S(1)}, /*index=5*/bf16[512,128]{1,0:T(8,128)(2,1)S(1)}, bf16[128,512]{1,0:T(8,128)(2,1)S(1)}, s32[]{:T(128)}) while((s32[]{:T(128)}, f32[128,512]{0,1:T(8,128)S(1)}, s32[]{:T(128)}, s32[512]{0:T(512)S(1)}, f32[512]{0:T(512)S(1)}, ...), condition=%wide.region_4.6_spmd, body=%wide.region_3.5_spmd.sunk | while | flops 135135744 | bytes 4199521 | solution.py:125
  172.7 2.3 while.39
  178.2 2.3 while.39
  183.6 2.3 while.39
  187.3 11.8 %gather_fusion.4 = f32[2048]{0:T(1024)S(1)} fusion(f32[2048]{0:T(1024)S(1)} %get-tuple-element.477, s32[2048]{0:T(1024)S(1)} %get-tuple-element.272), kind=kCustom, calls=%fused_computation.3.clone | custom fusion | bytes 24576 | tf_op jit(solution)/shard_map/jit(_take)/gather | solution.py:164
  199.1 5.5 %gather_fusion.3 = f32[2048,128]{1,0:T(8,128)S(1)} fusion(f32[128,2048]{0,1:T(8,128)S(1)} %copy-done.1, s32[2048]{0:T(1024)S(1)} %get-tuple-element.272), kind=kCustom, calls=%fused_computation.2.clone | custom fusion | bytes 2105344 | tf_op jit(solution)/shard_map/jit(_take)/gather | solution.py:164
  205.1 6.0 %all-to-all-start.4 = ((f32[64,1,1,1,1,128]{5,4,3,2,1,0:T(1,128)}), f32[64,1,1,1,1,128]{5,4,3,2,1,0:T(1,128)S(1)}, u32[]{:S(2)}, u32[]{:S(2)}) async-start(f32[64,1,1,1,1,128]{5,4,3,2,1,0:T(1,128)} %bitcast.49), calls=%async_computation.4 | async-start | bytes 65536 | tf_op jit(solution)/shard_map/all_to_all | solution.py:30
  213.3 14.6 %all-to-all-done.4 = f32[64,1,1,1,1,128]{5,4,3,2,1,0:T(1,128)S(1)} async-done(((f32[64,1,1,1,1,128]{5,4,3,2,1,0:T(1,128)}), f32[64,1,1,1,1,128]{5,4,3,2,1,0:T(1,128)S(1)}, u32[]{:S(2)}, u32[]{:S(2)}) %all-to-all-start.4) | async-done | bytes 32800 | tf_op jit(solution)/shard_map/all_to_all | solution.py:30
  228.0 5.5 %all-to-all-start.3 = ((f32[64,32,1,1,1,128]{5,1,4,3,2,0:T(8,128)}), f32[64,32,1,1,1,128]{5,1,4,3,2,0:T(8,128)}, u32[]{:S(2)}, u32[]{:S(2)}) async-start(f32[64,32,1,1,1,128]{5,1,4,3,2,0:T(8,128)} %bitcast.146), calls=%async_computation.3 | async-start | bytes 2097152 | tf_op jit(solution)/shard_map/all_to_all | solution.py:30
  238.9 49.9 %all-to-all-done.3 = f32[64,32,1,1,1,128]{5,1,4,3,2,0:T(8,128)} async-done(((f32[64,32,1,1,1,128]{5,1,4,3,2,0:T(8,128)}), f32[64,32,1,1,1,128]{5,1,4,3,2,0:T(8,128)}, u32[]{:S(2)}, u32[]{:S(2)}) %all-to-all-start.3) | async-done | bytes 1048608 | tf_op jit(solution)/shard_map/all_to_all | solution.py:30
  288.9 2.8 copy.71
  (154 shorter events, 48.5 us)
Async XLA Ops:
  0.6 18.1 %copy-start = (f32[32,4,16,128]{3,2,1,0:T(8,128)S(1)}, f32[32,4,16,128]{3,2,1,0:T(8,128)}, u32[]{:S(2)}) copy-start(f32[32,4,16,128]{3,2,1,0:T(8,128)} %param.18) | copy-start | bytes 3145732
  4.9 10.6 %all-to-all-start = ((f32[4,5,1,16,128]{4,3,2,1,0:T(8,128)}), f32[4,5,1,16,128]{4,3,2,1,0:T(8,128)S(1)}, u32[]{:S(2)}, u32[]{:S(2)}) async-start(f32[4,5,1,16,128]{4,3,2,1,0:T(8,128)} %stack.34), calls=%async_computation | async-start | bytes 327680 | tf_op jit(solution)/shard_map/all_to_all | solution.py:230
  16.7 2.0 copy-start.8
  16.8 2.1 copy-start.11
  16.8 2.1 copy-start.14
  19.7 58.0 %all-to-all-start.2 = ((f32[64,1,1,1,1,64]{5,4,3,2,1,0:T(1,128)}), f32[64,1,1,1,1,64]{5,4,3,2,1,0:T(1,128)}, u32[]{:S(2)}, u32[]{:S(2)}) async-start(f32[64,1,1,1,1,64]{5,4,3,2,1,0:T(1,128)} %bitcast.12), calls=%async_computation.2 | async-start | bytes 65536 | tf_op jit(solution)/shard_map/all_to_all | solution.py:30
  38.2 25.2 %collective-permute-start.1 = (f32[35,4,1,128]{3,2,1,0:T(1,128)}, f32[35,4,1,128]{3,2,1,0:T(1,128)}, u32[]{:S(2)}, u32[]{:S(2)}) collective-permute-start(f32[35,4,1,128]{3,2,1,0:T(1,128)} %get-tuple-element.253), channel_id=1, source_target_pairs={{0,8},{8,16},{16,24},{24,32},{32,40},{40,48},{48,56},{56,64},{64,7... | collective-permute-start | bytes 215048 | tf_op jit(solution)/shard_map/ppermute | solution.py:43
  42.2 21.1 %collective-permute-start.2 = (f32[35,4,1,128]{3,2,1,0:T(1,128)}, f32[35,4,1,128]{3,2,1,0:T(1,128)}, u32[]{:S(2)}, u32[]{:S(2)}) collective-permute-start(f32[35,4,1,128]{3,2,1,0:T(1,128)} %get-tuple-element.254), channel_id=1, source_target_pairs={{8,0},{16,8},{24,16},{32,24},{40,32},{48,40},{56,48},{64,56},{72,6... | collective-permute-start | bytes 215048 | tf_op jit(solution)/shard_map/ppermute | solution.py:44
  45.0 7.7 %copy-start.17 = (f32[3,16,128]{2,1,0:T(8,128)S(1)}, f32[3,16,128]{2,1,0:T(8,128)}, u32[]{:S(2)}) copy-start(f32[3,16,128]{2,1,0:T(8,128)} %get-tuple-element.260) | copy-start | bytes 73732
  45.0 7.7 %copy-start.18 = (f32[3,16,128]{2,1,0:T(8,128)S(1)}, f32[3,16,128]{2,1,0:T(8,128)}, u32[]{:S(2)}) copy-start(f32[3,16,128]{2,1,0:T(8,128)} %get-tuple-element.261) | copy-start | bytes 73732
  48.3 10.7 %collective-permute-start.3 = (f32[35,4,16,1]{0,2,3,1:T(8,128)}, f32[35,4,16,1]{0,2,3,1:T(8,128)}, u32[]{:S(2)}, u32[]{:S(2)}) collective-permute-start(f32[35,4,16,1]{0,2,3,1:T(8,128)} %copy.55), channel_id=1, source_target_pairs={{1,0},{2,1},{3,2},{4,3},{5,4},{6,5},{7,6},{9,8},{10,9},{11,10},{12... | collective-permute-start | bytes 26888 | tf_op jit(solution)/shard_map/ppermute | solution.py:44
  50.2 5.2 %collective-permute-start = (f32[35,4,16,1]{0,2,3,1:T(8,128)S(1)}, f32[35,4,16,1]{0,2,3,1:T(8,128)S(1)}, u32[]{:S(2)}, u32[]{:S(2)}) collective-permute-start(f32[35,4,16,1]{0,2,3,1:T(8,128)S(1)} %copy.53), channel_id=1, source_target_pairs={{0,1},{1,2},{2,3},{3,4},{4,5},{5,6},{6,7},{8,9},{9,10},{10,11},{11... | collective-permute-start | bytes 26888 | tf_op jit(solution)/shard_map/ppermute | solution.py:43
  59.0 9.5 %copy-start.4 = (f32[35,4,18,1]{3,2,1,0:T(8,128)}, f32[35,4,18,1]{3,2,1,0:T(8,128)S(1)}, u32[]{:S(2)}) copy-start(f32[35,4,18,1]{3,2,1,0:T(8,128)S(1)} %pad.9) | copy-start | bytes 30244
  61.8 1.6 copy-start.9
  61.8 1.6 copy-start.12
  61.8 1.6 copy-start.15
  63.4 5.1 %copy-start.6 = (f32[35,4,18,1]{3,2,1,0:T(8,128)}, f32[35,4,18,1]{3,2,1,0:T(8,128)S(1)}, u32[]{:S(2)}) copy-start(f32[35,4,18,1]{3,2,1,0:T(8,128)S(1)} %pad.10) | copy-start | bytes 30244
  77.7 77.9 %all-to-all-start.1 = ((f32[64,32,1,1,1,128]{5,1,4,3,2,0:T(8,128)}), f32[64,32,1,1,1,128]{5,1,4,3,2,0:T(8,128)S(1)}, u32[]{:S(2)}, u32[]{:S(2)}) async-start(f32[64,32,1,1,1,128]{5,1,4,3,2,0:T(8,128)} %copy.57), calls=%async_computation.1 | async-start | bytes 2097152 | tf_op jit(solution)/shard_map/all_to_all | solution.py:30
  161.4 2.4 copy-start.2
  161.4 2.4 copy-start.3
  161.4 2.4 copy-start.19
  187.3 11.8 %copy-start.1 = (f32[128,2048]{0,1:T(8,128)S(1)}, f32[128,2048]{0,1:T(8,128)}, u32[]{:S(2)}) copy-start(f32[128,2048]{0,1:T(8,128)} %get-tuple-element.476) | copy-start | bytes 3145732
  205.1 22.8 %all-to-all-start.4 = ((f32[64,1,1,1,1,128]{5,4,3,2,1,0:T(1,128)}), f32[64,1,1,1,1,128]{5,4,3,2,1,0:T(1,128)S(1)}, u32[]{:S(2)}, u32[]{:S(2)}) async-start(f32[64,1,1,1,1,128]{5,4,3,2,1,0:T(1,128)} %bitcast.49), calls=%async_computation.4 | async-start | bytes 65536 | tf_op jit(solution)/shard_map/all_to_all | solution.py:30
  212.0 21.5 %copy-start.10 = (f32[1,4,16,128]{3,2,1,0:T(8,128)S(1)}, f32[1,4,16,128]{3,2,1,0:T(8,128)}, u32[]{:S(2)}) copy-start(f32[1,4,16,128]{3,2,1,0:T(8,128)} %copy-done.8) | copy-start | bytes 98308
  212.0 21.5 %copy-start.13 = (f32[1,4,16,128]{3,2,1,0:T(8,128)S(1)}, f32[1,4,16,128]{3,2,1,0:T(8,128)}, u32[]{:S(2)}) copy-start(f32[1,4,16,128]{3,2,1,0:T(8,128)} %copy-done.11) | copy-start | bytes 98308
  212.0 21.5 %copy-start.16 = (f32[1,4,16,128]{3,2,1,0:T(8,128)S(1)}, f32[1,4,16,128]{3,2,1,0:T(8,128)}, u32[]{:S(2)}) copy-start(f32[1,4,16,128]{3,2,1,0:T(8,128)} %copy-done.14) | copy-start | bytes 98308
  213.3 20.3 %copy-start.5 = (f32[35,4,18,1]{3,2,1,0:T(8,128)S(1)}, f32[35,4,18,1]{3,2,1,0:T(8,128)}, u32[]{:S(2)}) copy-start(f32[35,4,18,1]{3,2,1,0:T(8,128)} %copy-done.4) | copy-start | bytes 30244
  228.0 60.9 %all-to-all-start.3 = ((f32[64,32,1,1,1,128]{5,1,4,3,2,0:T(8,128)}), f32[64,32,1,1,1,128]{5,1,4,3,2,0:T(8,128)}, u32[]{:S(2)}, u32[]{:S(2)}) async-start(f32[64,32,1,1,1,128]{5,1,4,3,2,0:T(8,128)} %bitcast.146), calls=%async_computation.3 | async-start | bytes 2097152 | tf_op jit(solution)/shard_map/all_to_all | solution.py:30
  233.6 2.6 copy-start.7
